TPU v7x, 256 devices: a whole 4x4x8 slice. The times are simulated.
256 devices in a mesh: seq: 32 (over x, z), tp: 4 (over y), lat: 2 (over core).
Axes of the slice: x: 4, y: 4, z: 8, core: 2. Of those that a mesh axis runs over, the one named last changes fastest.
Arguments:
- tokens: bfloat16 [24576, 8192], P(('seq', 'lat'), 'tp'), may hold values from -6 to 6
- active: int32 [24576, 4], P(('seq', 'lat')), may hold values from 0 to 255, all different within a row; in each aligned block of 384 rows (0 to 383, 384 to 767, ...) at most 9 rows name the same one
- placement_map: int32 [256], replicated, may hold values from 0 to 255, each once
- enc_weight: bfloat16 [8192, 32768], P('tp', ('seq', 'lat')), may hold values from -0.0625 to 0.0625
- enc_bias: float32 [32768], P(('seq', 'lat')), may hold values from -3 to 3
- dec_weight: bfloat16 [32768, 8192], P(('seq', 'lat'), 'tp'), may hold values from -0.375 to 0.375
- dec_bias: float32 [8192], P('tp'), may hold values from -3 to 3
Outputs:
- recon: bfloat16 [24576, 8192], P(('seq', 'lat'), 'tp')
Inputs may be any that keep to these rules, and one draw needn't show every extreme that they name: `active`: the 4 blocks of one token are different. Among the rows of one device (aligned blocks of 384 rows) no block is named more than 9 times, and some block is named exactly 9 times. `placement_map`: each column block appears once.
All inputs are finite; a program needn't handle non-finite values.
Results may differ from a plain program's by a relative error of at most 0.0061.
Values may be sent and summed in bfloat16 or wider, within the bound.
A program may use at most 128 MiB of HBM per device.

v0:
```python
import jax
import jax.numpy as jnp
from jax import lax
from jax.sharding import PartitionSpec as P


def local(tokens, active, placement_map, enc_weight, enc_bias, dec_weight, dec_bias):
    rows, width = tokens.shape
    top = active.shape[1]
    nblocks = placement_map.shape[0]
    seq_count = lax.axis_size("seq")
    lat_count = lax.axis_size("lat")
    owners = seq_count * lat_count
    local_blocks = nblocks // owners
    block_width = enc_bias.shape[0] // local_blocks
    capacity = 3 * rows * top // (2 * nblocks)
    centered = (tokens.astype(jnp.float32) - dec_bias[None, :]).astype(jnp.bfloat16)
    block_ids = jnp.arange(nblocks, dtype=jnp.int32)
    matches = (active[:, :, None] == block_ids[None, None, :]).astype(jnp.int32)
    position = jnp.sum(matches * placement_map[None, None, :], axis=2).reshape(-1)
    pos_hot = (position[:, None] == block_ids[None, :]).astype(jnp.int32)
    rank = jnp.sum((jnp.cumsum(pos_hot, axis=0) - 1) * pos_hot, axis=1)
    target = position * capacity + rank
    pair_row = jnp.arange(rows * top, dtype=jnp.int32) // top
    slot_row = jnp.zeros((nblocks * capacity,), jnp.int32).at[target].set(pair_row)
    filled = jnp.zeros((nblocks * capacity,), jnp.bool_).at[target].set(True)
    outgoing = jnp.where(filled[:, None], centered[slot_row], jnp.zeros((), jnp.bfloat16))
    outgoing = outgoing.reshape(owners, local_blocks, capacity, width)
    enc_blocks = enc_weight.reshape(width, local_blocks, block_width)
    bias_blocks = enc_bias.reshape(local_blocks, block_width)
    dec_blocks = dec_weight.reshape(local_blocks, block_width, width)
    preact = jnp.einsum(
        "sbcd,dbh->sbch",
        lax.all_to_all(outgoing, ("seq", "lat"), split_axis=0, concat_axis=0, tiled=True),
        enc_blocks,
        preferred_element_type=jnp.float32,
    )
    summed = lax.psum(preact, "tp")
    codes = jnp.maximum(summed + bias_blocks[None, :, None, :], 0.0).astype(jnp.bfloat16)
    returned = lax.all_to_all(
        jnp.einsum("sbch,bhd->sbcd", codes, dec_blocks, preferred_element_type=jnp.float32).astype(
            jnp.bfloat16
        ),
        ("seq", "lat"),
        split_axis=0,
        concat_axis=0,
        tiled=True,
    )
    returned = returned.reshape(nblocks * capacity, width)
    contrib = returned[target].reshape(rows, top, width).astype(jnp.float32)
    return (jnp.sum(contrib, axis=1) + dec_bias[None, :]).astype(jnp.bfloat16)


def solution(mesh):
    return jax.shard_map(
        local,
        mesh=mesh,
        in_specs=(
            P(("seq", "lat"), "tp"),
            P(("seq", "lat"), None),
            P(),
            P("tp", ("seq", "lat")),
            P(("seq", "lat")),
            P(("seq", "lat"), "tp"),
            P("tp"),
        ),
        out_specs=P(("seq", "lat"), "tp"),
        check_vma=False,
    )
```

profile of v0, /device:TPU:1, one launch (start us, length us, event | category | flops | bytes accessed | tf_op | source)
XLA Modules:
  0.0 689.2 jit_solution(1939051492768150350)
XLA Ops:
  6.5 0.0 copy-start
  6.5 1.4 select_reduce_fusion
  7.9 0.1 copy.29
  8.0 0.1 eq.45
  8.2 0.1 eq.41
  8.4 0.1 copy.31
  8.5 0.3 fusion.3
  8.8 0.0 copy-start.2
  8.8 1.3 copy-done.2
  10.2 1.8 add_add_fusion
  12.0 0.0 copy-start.3
  12.1 2.1 copy.32
  14.1 0.1 copy.28
  14.3 0.2 mul.31
  14.4 1.9 fusion.5
  16.4 6.4 scatter_custom_fusion.1
  22.8 0.0 copy-done.3
  22.8 2.9 subtract_convert_fusion
  25.7 20.0 %gather_fusion = bf16[2304,2048]{1,0:T(8,128)(2,1)} fusion(bf16[384,2048]{1,0:T(8,128)(2,1)} %subtract_convert_fusion, s32[3072]{0:T(1024)S(1)} %pad_clamp_fusion), kind=kCustom, calls=%fused_computation | custom fusion | bytes 18883584 | tf_op jit(solution)/shard_map/gather | solution.py:27
  45.7 15.1 %gather.9 = bf16[64,4,9,2048]{3,2,1,0:T(8,128)(2,1)} reshape(bf16[2304,2048]{1,0:T(8,128)(2,1)} %gather_fusion) | data formatting | bytes 18874368 | tf_op jit(solution)/shard_map/gather | solution.py:27
  60.8 11.2 %scatter_custom_fusion = pred[2304]{0:T(1024)(128)(4,1)S(1)} fusion(s32[1536]{0:T(1024)S(1)} %fusion.17, pred[1536]{0:T(1024)(128)(4,1)S(1)} %broadcast.82, pred[]{:T(512)} %constant.16.clone.1), kind=kCustom, calls=%fused_computation.40 | custom fusion | bytes 2305 | tf_op jit(solution)/shard_map/scatter | solution.py:26
  72.0 0.2 broadcast_in_dim.35
  72.2 8.3 %broadcast_select_fusion = bf16[64,4,9,2048]{3,2,1,0:T(8,128)(2,1)S(1)} fusion(bf16[64,4,9,2048]{3,2,1,0:T(8,128)(2,1)} %gather.9, pred[64,4,9]{2,1,0:T(4,128)(4,1)S(1)} %broadcast_in_dim.35), kind=kLoop, calls=%fused_computation.4 | loop fusion | flops 4718592 | bytes 18876672 | tf_op jit(solution)/shard_map/jit(_where)/select_n | solution.py:27
  80.5 19.6 %copy.33 = bf16[64,4,9,2048]{3,1,2,0:T(4,128)(2,1)} copy(bf16[64,4,9,2048]{3,2,1,0:T(8,128)(2,1)S(1)} %broadcast_select_fusion) | data formatting | bytes 18874368 | tf_op jit(solution)/shard_map/jit(_where)/select_n | solution.py:27
  100.1 13.2 %all-to-all-start = ((bf16[64,4,9,2048]{3,1,2,0:T(4,128)(2,1)}), bf16[64,4,9,2048]{3,1,2,0:T(4,128)(2,1)}, u32[]{:S(2)}, u32[]{:S(2)}) async-start(bf16[64,4,9,2048]{3,1,2,0:T(4,128)(2,1)} %copy.33), calls=%async_computation | async-start | bytes 18874368 | tf_op jit(solution)/shard_map/all_to_all | solution.py:34
  113.2 0.3 all-reduce.2.cloned.1.call-start
  113.5 4.0 reshape.73
  117.5 204.0 %all-to-all-done = bf16[64,4,9,2048]{3,1,2,0:T(4,128)(2,1)} async-done(((bf16[64,4,9,2048]{3,1,2,0:T(4,128)(2,1)}), bf16[64,4,9,2048]{3,1,2,0:T(4,128)(2,1)}, u32[]{:S(2)}, u32[]{:S(2)}) %all-to-all-start) | async-done | bytes 9437216 | tf_op jit(solution)/shard_map/all_to_all | solution.py:34
  321.5 0.0 copy-start.4
  321.5 10.5 %fusion.6 = f32[64,4,9,128]{3,0,2,1:T(8,128)} fusion(bf16[2048,4,128,1]{2,1,0,3:T(4,128)(2,1)} %bitcast.22, bf16[64,4,9,2048]{3,1,2,0:T(4,128)(2,1)} %all-to-all-done), kind=kOutput, calls=%fused_computation.20 | convolution fusion | flops 1207959552 | bytes 12713984 | tf_op jit(solution)/shard_map/sbcd,dbh->sbch/dot_general | solution.py:32
  332.0 0.0 all-reduce.2.cloned.1.call-update
  332.0 47.5 %all-reduce.2.cloned.1.call-done = f32[64,4,9,128]{3,0,2,1:T(8,128)} async-done(((f32[64,4,9,128]{3,0,2,1:T(8,128)}), f32[64,4,9,128]{3,0,2,1:T(8,128)}) %all-reduce.2.cloned.1.call-update) | async-done | bytes 1179664 | tf_op jit(solution)/shard_map/psum | solution.py:38
  379.5 0.0 copy-done
  379.5 0.0 copy-done.4
  379.5 4.1 convert_bitcast_fusion
  383.6 7.3 %copy.36 = bf16[64,4,9,2048]{3,1,2,0:T(4,128)(2,1)} copy(bf16[64,4,9,2048]{3,0,2,1:T(8,128)(2,1)S(1)} %convert_bitcast_fusion) | data formatting | bytes 18874368 | tf_op jit(solution)/shard_map/convert_element_type | solution.py:41
  390.9 11.9 %all-to-all-start.1 = ((bf16[64,4,9,2048]{3,1,2,0:T(4,128)(2,1)}), bf16[64,4,9,2048]{3,1,2,0:T(4,128)(2,1)}, u32[]{:S(2)}, u32[]{:S(2)}) async-start(bf16[64,4,9,2048]{3,1,2,0:T(4,128)(2,1)} %copy.36), calls=%async_computation.1 | async-start | bytes 18874368 | tf_op jit(solution)/shard_map/all_to_all | solution.py:40
  402.9 208.2 %all-to-all-done.1 = bf16[64,4,9,2048]{3,1,2,0:T(4,128)(2,1)} async-done(((bf16[64,4,9,2048]{3,1,2,0:T(4,128)(2,1)}), bf16[64,4,9,2048]{3,1,2,0:T(4,128)(2,1)}, u32[]{:S(2)}, u32[]{:S(2)}) %all-to-all-start.1) | async-done | bytes 9437216 | tf_op jit(solution)/shard_map/all_to_all | solution.py:40
  611.1 10.7 %copy.37 = bf16[64,4,9,2048]{3,2,1,0:T(8,128)(2,1)} copy(bf16[64,4,9,2048]{3,1,2,0:T(4,128)(2,1)} %all-to-all-done.1) | data formatting | bytes 18874368 | tf_op jit(solution)/shard_map/all_to_all | solution.py:40
  621.8 15.8 %reshape.75 = bf16[2304,2048]{1,0:T(8,128)(2,1)} reshape(bf16[64,4,9,2048]{3,2,1,0:T(8,128)(2,1)} %copy.37) | data formatting | bytes 18874368 | tf_op jit(solution)/shard_map/reshape | solution.py:49
  637.6 17.6 %gather_fusion.1 = bf16[1536,2048]{1,0:T(8,128)(2,1)} fusion(bf16[2304,2048]{1,0:T(8,128)(2,1)} %reshape.75, s32[2048]{0:T(1024)S(1)} %pad_clamp_fusion.1), kind=kCustom, calls=%fused_computation.1 | custom fusion | bytes 12589056 | tf_op jit(solution)/shard_map/gather | solution.py:50
  655.2 11.9 %reshape.76 = f32[384,4,2048]{2,1,0:T(4,128)} reshape(bf16[1536,2048]{1,0:T(8,128)(2,1)} %gather_fusion.1) | data formatting | bytes 18874368 | tf_op jit(solution)/shard_map/convert_element_type | solution.py:50
  667.1 0.0 copy-start.1
  667.1 11.9 %reduce_sum.32 = f32[384,2048]{1,0:T(8,128)} reduce(f32[384,4,2048]{2,1,0:T(4,128)} %reshape.76, f32[]{:T(128)} %constant.42.clone.1), dimensions={1}, to_apply=%region_7.8 | reduce | flops 2359296 | bytes 15728644 | tf_op jit(solution)/shard_map/reduce_sum | solution.py:51
  679.0 3.4 add_convert_fusion
  682.4 0.0 copy-done.1
  (9 shorter events, 0.1 us)
Async XLA Ops:
  6.5 373.0 %copy-start = (bf16[512,2048]{1,0:T(8,128)(2,1)S(1)}, bf16[512,2048]{1,0:T(8,128)(2,1)}, u32[]{:S(2)}) copy-start(bf16[512,2048]{1,0:T(8,128)(2,1)} %param.12) | copy-start | bytes 6291460
  8.8 1.4 copy-start.2
  12.0 10.7 %copy-start.3 = (f32[2048]{0:T(1024)S(1)}, f32[2048]{0:T(1024)}, u32[]{:S(2)}) copy-start(f32[2048]{0:T(1024)} %param.13) | copy-start | bytes 24580
  100.1 221.4 %all-to-all-start = ((bf16[64,4,9,2048]{3,1,2,0:T(4,128)(2,1)}), bf16[64,4,9,2048]{3,1,2,0:T(4,128)(2,1)}, u32[]{:S(2)}, u32[]{:S(2)}) async-start(bf16[64,4,9,2048]{3,1,2,0:T(4,128)(2,1)} %copy.33), calls=%async_computation | async-start | bytes 18874368 | tf_op jit(solution)/shard_map/all_to_all | solution.py:34
  113.2 266.3 %all-reduce.2.cloned.1.call-start = ((), (), s32[]{:S(2)}) async-start(), calls=%async_computation.2 | async-start | bytes 2359296 | tf_op jit(solution)/shard_map/psum | solution.py:38
  321.5 58.0 %copy-start.4 = (f32[512]{0:T(512)S(1)}, f32[512]{0:T(512)}, u32[]{:S(2)}) copy-start(f32[512]{0:T(512)} %param.11) | copy-start | bytes 6148
  390.9 220.2 %all-to-all-start.1 = ((bf16[64,4,9,2048]{3,1,2,0:T(4,128)(2,1)}), bf16[64,4,9,2048]{3,1,2,0:T(4,128)(2,1)}, u32[]{:S(2)}, u32[]{:S(2)}) async-start(bf16[64,4,9,2048]{3,1,2,0:T(4,128)(2,1)} %copy.36), calls=%async_computation.1 | async-start | bytes 18874368 | tf_op jit(solution)/shard_map/all_to_all | solution.py:40
  667.1 15.3 %copy-start.1 = (bf16[512,2048]{1,0:T(8,128)(2,1)S(1)}, bf16[512,2048]{1,0:T(8,128)(2,1)}, u32[]{:S(2)}) copy-start(bf16[512,2048]{1,0:T(8,128)(2,1)} %param.12) | copy-start | bytes 6291460
Sparse Core Ops, SparseCore 0:
  332.1 47.3 all-reduce.1
where the time goes:
time: 691 us; the launch traced here: 689 us
  waiting for transfers between devices  460 us (67%)
  local copies, waits for them, and re-layouts  144 us (21%)
  other arithmetic  32 us (5%)
  starting transfers between devices  25.3 us (4%)
  matrix products  14.6 us (2%)
  between operations  13.6 us (2%)
    all_to_all x1, waiting for transfers between devices, local(): lax.all_to_all(jnp.einsum('sbch,bhd->sbcd', codes, dec_blocks, preferred_...  208 us
    all_to_all x1, waiting for transfers between devices, local(): lax.all_to_all(outgoing, ('seq', 'lat'), split_axis=0, concat_axis=0, til...  204 us
    psum x1, waiting for transfers between devices, local(): summed = lax.psum(preact, 'tp')  47.5 us
    gather x2, local copies, waits for them, and re-layouts, local(): centered[slot_row]  35 us
    select_n x1, local copies, waits for them, and re-layouts, local(): jnp.where(filled[:, None], centered[slot_row], jnp.zeros((), jnp.bfloat16))  19.6 us
    gather x1, local copies, waits for them, and re-layouts, local(): contrib = returned[target].reshape(rows, top, width).astype(jnp.float32)  17.6 us
    reshape x1, local copies, waits for them, and re-layouts, local(): returned = returned.reshape(nblocks * capacity, width)  15.8 us
  transfers between devices with their start and end apart: 3, of which 3 were waited for; matrix products, arithmetic and copies ran while one was open for 1% of the time, Pallas kernels for 0%

commit v1 on v0

--- a/solution.py
+++ b/solution.py
@@ -35,7 +35,7 @@
         enc_blocks,
         preferred_element_type=jnp.float32,
     )
-    summed = lax.psum(preact, "tp")
+    summed = jnp.sum(lax.all_gather(preact, "tp"), axis=0)
     codes = jnp.maximum(summed + bias_blocks[None, :, None, :], 0.0).astype(jnp.bfloat16)
     returned = lax.all_to_all(
         jnp.einsum("sbch,bhd->sbcd", codes, dec_blocks, preferred_element_type=jnp.float32).astype(

time: 691 us -> 696 us (level)
    all_gather x0 -> x1, waiting for transfers between devices: none -> 52.1 us  [local(): summed = jnp.sum(lax.all_gather(preact, 'tp'), axis=0)]
    psum x1 -> x0, waiting for transfers between devices: 47.5 us -> none  [local(): summed = lax.psum(preact, 'tp')]
where the time goes in v1:
time: 696 us; the launch traced here: 694 us
  waiting for transfers between devices  464 us (67%)
  local copies, waits for them, and re-layouts  144 us (21%)
  other arithmetic  35 us (5%)
  starting transfers between devices  24.2 us (3%)
  between operations  13.6 us (2%)
  matrix products  13.3 us (2%)
    all_to_all x1, waiting for transfers between devices, local(): lax.all_to_all(jnp.einsum('sbch,bhd->sbcd', codes, dec_blocks, preferred_...  208 us
    all_to_all x1, waiting for transfers between devices, local(): lax.all_to_all(outgoing, ('seq', 'lat'), split_axis=0, concat_axis=0, til...  204 us
    all_gather x1, waiting for transfers between devices, local(): summed = jnp.sum(lax.all_gather(preact, 'tp'), axis=0)  52.1 us
    gather x2, local copies, waits for them, and re-layouts, local(): centered[slot_row]  35 us
    select_n x1, local copies, waits for them, and re-layouts, local(): jnp.where(filled[:, None], centered[slot_row], jnp.zeros((), jnp.bfloat16))  19.6 us
    gather x1, local copies, waits for them, and re-layouts, local(): contrib = returned[target].reshape(rows, top, width).astype(jnp.float32)  17.6 us
    reshape x1, local copies, waits for them, and re-layouts, local(): returned = returned.reshape(nblocks * capacity, width)  15.8 us
  transfers between devices with their start and end apart: 3, of which 3 were waited for; matrix products, arithmetic and copies ran while one was open for 1% of the time, Pallas kernels for 0%

profile of v1, /device:TPU:1, one launch (start us, length us, event | category | flops | bytes accessed | tf_op | source)
XLA Modules:
  0.0 694.4 jit_solution(4448962011942635407)
XLA Ops:
  6.5 0.0 copy-start
  6.5 1.4 select_reduce_fusion
  7.9 0.1 copy.32
  8.0 0.1 eq.45
  8.2 0.1 eq.41
  8.4 0.1 copy.34
  8.5 0.3 fusion.3
  8.8 0.0 copy-start.2
  8.8 1.3 copy-done.2
  10.2 1.8 add_add_fusion
  12.0 0.0 copy-start.3
  12.1 2.1 copy.35
  14.1 0.1 copy.31
  14.3 0.2 mul.31
  14.4 1.9 fusion.5
  16.4 6.4 scatter_custom_fusion.1
  22.8 0.0 copy-done.3
  22.8 2.9 subtract_convert_fusion
  25.7 20.0 %gather_fusion = bf16[2304,2048]{1,0:T(8,128)(2,1)} fusion(bf16[384,2048]{1,0:T(8,128)(2,1)} %subtract_convert_fusion, s32[3072]{0:T(1024)S(1)} %pad_clamp_fusion), kind=kCustom, calls=%fused_computation | custom fusion | bytes 18883584 | tf_op jit(solution)/shard_map/gather | solution.py:27
  45.7 15.1 %gather.9 = bf16[64,4,9,2048]{3,2,1,0:T(8,128)(2,1)} reshape(bf16[2304,2048]{1,0:T(8,128)(2,1)} %gather_fusion) | data formatting | bytes 18874368 | tf_op jit(solution)/shard_map/gather | solution.py:27
  60.8 11.2 %scatter_custom_fusion = pred[2304]{0:T(1024)(128)(4,1)S(1)} fusion(s32[1536]{0:T(1024)S(1)} %fusion.17, pred[1536]{0:T(1024)(128)(4,1)S(1)} %broadcast.82, pred[]{:T(512)} %constant.16.clone.1), kind=kCustom, calls=%fused_computation.40 | custom fusion | bytes 2305 | tf_op jit(solution)/shard_map/scatter | solution.py:26
  72.0 0.2 broadcast_in_dim.35
  72.2 8.3 %broadcast_select_fusion = bf16[64,4,9,2048]{3,2,1,0:T(8,128)(2,1)S(1)} fusion(bf16[64,4,9,2048]{3,2,1,0:T(8,128)(2,1)} %gather.9, pred[64,4,9]{2,1,0:T(4,128)(4,1)S(1)} %broadcast_in_dim.35), kind=kLoop, calls=%fused_computation.4 | loop fusion | flops 4718592 | bytes 18876672 | tf_op jit(solution)/shard_map/jit(_where)/select_n | solution.py:27
  80.5 19.6 %copy.36 = bf16[64,4,9,2048]{3,1,2,0:T(4,128)(2,1)} copy(bf16[64,4,9,2048]{3,2,1,0:T(8,128)(2,1)S(1)} %broadcast_select_fusion) | data formatting | bytes 18874368 | tf_op jit(solution)/shard_map/jit(_where)/select_n | solution.py:27
  100.1 13.2 %all-to-all-start = ((bf16[64,4,9,2048]{3,1,2,0:T(4,128)(2,1)}), bf16[64,4,9,2048]{3,1,2,0:T(4,128)(2,1)}, u32[]{:S(2)}, u32[]{:S(2)}) async-start(bf16[64,4,9,2048]{3,1,2,0:T(4,128)(2,1)} %copy.36), calls=%async_computation | async-start | bytes 18874368 | tf_op jit(solution)/shard_map/all_to_all | solution.py:34
  113.2 0.3 all-gather.3.cloned.1.call-start
  113.5 4.0 reshape.73
  117.5 204.0 %all-to-all-done = bf16[64,4,9,2048]{3,1,2,0:T(4,128)(2,1)} async-done(((bf16[64,4,9,2048]{3,1,2,0:T(4,128)(2,1)}), bf16[64,4,9,2048]{3,1,2,0:T(4,128)(2,1)}, u32[]{:S(2)}, u32[]{:S(2)}) %all-to-all-start) | async-done | bytes 9437216 | tf_op jit(solution)/shard_map/all_to_all | solution.py:34
  321.5 10.5 %fusion.6 = f32[64,4,9,128]{3,0,2,1:T(8,128)} fusion(bf16[2048,4,128,1]{2,1,0,3:T(4,128)(2,1)} %bitcast.24, bf16[64,4,9,2048]{3,1,2,0:T(4,128)(2,1)} %all-to-all-done), kind=kOutput, calls=%fused_computation.20 | convolution fusion | flops 1207959552 | bytes 12713984 | tf_op jit(solution)/shard_map/sbcd,dbh->sbch/dot_general | solution.py:32
  332.0 0.0 all-gather.3.cloned.1.call-update
  332.0 52.1 %all-gather.3.cloned.1.call-done = f32[256,4,9,128]{3,0,2,1:T(8,128)} async-done(((f32[64,4,9,128]{3,0,2,1:T(8,128)}), f32[256,4,9,128]{3,0,2,1:T(8,128)}) %all-gather.3.cloned.1.call-update) | async-done | bytes 4718608 | tf_op jit(solution)/shard_map/all_gather | solution.py:38
  384.1 0.0 copy-start.4
  384.1 3.0 reduce_sum.41
  387.1 0.0 copy-done
  387.1 0.0 copy-done.4
  387.1 2.8 convert_bitcast_fusion
  389.9 7.3 %copy.39 = bf16[64,4,9,2048]{3,1,2,0:T(4,128)(2,1)} copy(bf16[64,4,9,2048]{3,0,2,1:T(8,128)(2,1)S(1)} %convert_bitcast_fusion) | data formatting | bytes 18874368 | tf_op jit(solution)/shard_map/convert_element_type | solution.py:41
  397.3 10.8 %all-to-all-start.1 = ((bf16[64,4,9,2048]{3,1,2,0:T(4,128)(2,1)}), bf16[64,4,9,2048]{3,1,2,0:T(4,128)(2,1)}, u32[]{:S(2)}, u32[]{:S(2)}) async-start(bf16[64,4,9,2048]{3,1,2,0:T(4,128)(2,1)} %copy.39), calls=%async_computation.1 | async-start | bytes 18874368 | tf_op jit(solution)/shard_map/all_to_all | solution.py:40
  408.1 208.2 %all-to-all-done.1 = bf16[64,4,9,2048]{3,1,2,0:T(4,128)(2,1)} async-done(((bf16[64,4,9,2048]{3,1,2,0:T(4,128)(2,1)}), bf16[64,4,9,2048]{3,1,2,0:T(4,128)(2,1)}, u32[]{:S(2)}, u32[]{:S(2)}) %all-to-all-start.1) | async-done | bytes 9437216 | tf_op jit(solution)/shard_map/all_to_all | solution.py:40
  616.4 10.7 %copy.40 = bf16[64,4,9,2048]{3,2,1,0:T(8,128)(2,1)} copy(bf16[64,4,9,2048]{3,1,2,0:T(4,128)(2,1)} %all-to-all-done.1) | data formatting | bytes 18874368 | tf_op jit(solution)/shard_map/all_to_all | solution.py:40
  627.1 15.8 %reshape.75 = bf16[2304,2048]{1,0:T(8,128)(2,1)} reshape(bf16[64,4,9,2048]{3,2,1,0:T(8,128)(2,1)} %copy.40) | data formatting | bytes 18874368 | tf_op jit(solution)/shard_map/reshape | solution.py:49
  642.9 17.6 %gather_fusion.1 = bf16[1536,2048]{1,0:T(8,128)(2,1)} fusion(bf16[2304,2048]{1,0:T(8,128)(2,1)} %reshape.75, s32[2048]{0:T(1024)S(1)} %pad_clamp_fusion.1), kind=kCustom, calls=%fused_computation.1 | custom fusion | bytes 12589056 | tf_op jit(solution)/shard_map/gather | solution.py:50
  660.5 11.9 %reshape.76 = f32[384,4,2048]{2,1,0:T(4,128)} reshape(bf16[1536,2048]{1,0:T(8,128)(2,1)} %gather_fusion.1) | data formatting | bytes 18874368 | tf_op jit(solution)/shard_map/convert_element_type | solution.py:50
  672.3 0.0 copy-start.1
  672.3 11.9 %reduce_sum.42 = f32[384,2048]{1,0:T(8,128)} reduce(f32[384,4,2048]{2,1,0:T(4,128)} %reshape.76, f32[]{:T(128)} %constant.42.clone.1), dimensions={1}, to_apply=%region_7.8 | reduce | flops 2359296 | bytes 15728644 | tf_op jit(solution)/shard_map/reduce_sum | solution.py:51
  684.2 3.4 add_convert_fusion
  687.6 0.0 copy-done.1
  (9 shorter events, 0.1 us)
Async XLA Ops:
  6.5 380.6 %copy-start = (bf16[512,2048]{1,0:T(8,128)(2,1)S(1)}, bf16[512,2048]{1,0:T(8,128)(2,1)}, u32[]{:S(2)}) copy-start(bf16[512,2048]{1,0:T(8,128)(2,1)} %param.12) | copy-start | bytes 6291460
  8.8 1.4 copy-start.2
  12.0 10.7 %copy-start.3 = (f32[2048]{0:T(1024)S(1)}, f32[2048]{0:T(1024)}, u32[]{:S(2)}) copy-start(f32[2048]{0:T(1024)} %param.13) | copy-start | bytes 24580
  100.1 221.4 %all-to-all-start = ((bf16[64,4,9,2048]{3,1,2,0:T(4,128)(2,1)}), bf16[64,4,9,2048]{3,1,2,0:T(4,128)(2,1)}, u32[]{:S(2)}, u32[]{:S(2)}) async-start(bf16[64,4,9,2048]{3,1,2,0:T(4,128)(2,1)} %copy.36), calls=%async_computation | async-start | bytes 18874368 | tf_op jit(solution)/shard_map/all_to_all | solution.py:34
  113.2 270.9 %all-gather.3.cloned.1.call-start = ((), (), s32[]{:S(2)}) async-start(), calls=%async_computation.2 | async-start | bytes 5898240 | tf_op jit(solution)/shard_map/all_gather | solution.py:38
  384.1 3.0 copy-start.4
  397.3 219.1 %all-to-all-start.1 = ((bf16[64,4,9,2048]{3,1,2,0:T(4,128)(2,1)}), bf16[64,4,9,2048]{3,1,2,0:T(4,128)(2,1)}, u32[]{:S(2)}, u32[]{:S(2)}) async-start(bf16[64,4,9,2048]{3,1,2,0:T(4,128)(2,1)} %copy.39), calls=%async_computation.1 | async-start | bytes 18874368 | tf_op jit(solution)/shard_map/all_to_all | solution.py:40
  672.3 15.3 %copy-start.1 = (bf16[512,2048]{1,0:T(8,128)(2,1)S(1)}, bf16[512,2048]{1,0:T(8,128)(2,1)}, u32[]{:S(2)}) copy-start(bf16[512,2048]{1,0:T(8,128)(2,1)} %param.12) | copy-start | bytes 6291460
Sparse Core Ops, SparseCore 0:
  332.1 51.9 all-gather.2
